TPU v7x, 256 devices: a whole 4x4x8 slice. The times are simulated.
256 devices in a mesh: dp: 4 (over y), tensor: 16 (over x_hi, z), rep: 4 (over x_lo, core).
Axes of the slice: x: 4 (x_hi: 2, x_lo: 2; x = x_hi * 2 + x_lo), y: 4, z: 8, core: 2. Of those that a mesh axis runs over, the one named last changes fastest.
Arguments:
- resid: bfloat16 [512, 8192], P('dp', 'rep'), may hold values from -94 to 94
- norm_gain: float32 [8192], P('rep'), may hold values from 0.25 to 1.75
- gate_weight: bfloat16 [4, 2048, 14336], P('rep', 'dp', 'tensor'), may hold values from -0.0625 to 0.0625
- up_weight: bfloat16 [4, 2048, 14336], P('rep', 'dp', 'tensor'), may hold values from -0.0625 to 0.0625
- down_weight: bfloat16 [14336, 4, 2048], P('tensor', 'rep', 'dp'), may hold values from -0.046875 to 0.046875
- enc_weight: bfloat16 [8192, 65536], P('rep', ('dp', 'tensor')), may hold values from -0.0625 to 0.0625
- enc_bias: float32 [65536], P(('dp', 'tensor')), may hold values from -3 to 3
- dec_weight: bfloat16 [65536, 8192], P(('dp', 'tensor'), 'rep'), may hold values from -1 to 1
- dec_bias: float32 [8192], P('rep'), may hold values from -3 to 3
- latent_ids: int32 [512, 64], replicated, may hold values from 0 to 65535, as said below
Outputs:
- resid_out: bfloat16 [512, 8192], P(('dp', 'tensor'), 'rep')
- recon: bfloat16 [512, 8192], P(('dp', 'tensor'), 'rep')
- error_ratio: float32 [512], P(('dp', 'tensor'))
Inputs may be any that keep to these rules, and one draw needn't show every extreme that they name: `latent_ids`: each row names 64 distinct latents: 8 latents in each of 8 distinct blocks of 128 consecutive latents (block b holds latents b * 128 to b * 128 + 127).
All inputs are finite; a program needn't handle non-finite values.
Results may differ from a plain program's by a relative error of at most 0.009.
Values may be sent and summed in bfloat16 or wider, within the bound.
No kernel may reach another device: no remote copies, remote signals or barrier semaphores. Data moves between devices by JAX's collectives and lax.ppermute only.
A program may use at most 64 MiB of HBM per device.

v0:
```python
import jax
import jax.numpy as jnp
from jax import lax
from jax.experimental import pallas as pl
from jax.experimental.pallas import tpu as pltpu
from jax.sharding import Mesh, PartitionSpec as P

BF = jnp.bfloat16
F32 = jnp.float32
I32 = jnp.int32
VM = pl.BlockSpec(memory_space=pltpu.VMEM)
SM = pl.BlockSpec(memory_space=pltpu.SMEM)
ANY = pl.BlockSpec(memory_space=pltpu.HBM)
MIB = 1 << 20


def call(kernel, outs, n_in, scratch, flops, nbytes, limit=12, any_at=(), any_out=False):
    in_specs = [SM] + [ANY if i in any_at else VM for i in range(n_in)]
    return pl.pallas_call(
        kernel,
        out_shape=outs,
        in_specs=in_specs,
        out_specs=jax.tree.map(lambda _: ANY if any_out else VM, outs),
        scratch_shapes=scratch,
        compiler_params=pltpu.CompilerParams(vmem_limit_bytes=limit * MIB),
        cost_estimate=pl.CostEstimate(flops=flops, bytes_accessed=nbytes, transcendentals=0),
    )


def sds(shape, dt):
    return jax.ShapeDtypeStruct(shape, dt)


def mm(a, b):
    return jnp.dot(a, b, preferred_element_type=F32)


SEATS = 64
ROWS = 4 * SEATS


def gate_kernel(pos, p0, p1, p2, p3, gain, go, gp, *refs):
    outs, xsel, xg, pk, xr = refs[:4], refs[4], refs[5], refs[6], refs[7]
    for s, part in enumerate((p0, p1, p2, p3)):
        xr[s * 64:(s + 1) * 64, :] = part[...].astype(F32)
    xf = xr[...]
    xg[...] = (xf * gain[...]).astype(BF)
    ss = jnp.sum(xf * xf, axis=1, keepdims=True)
    hi = ss.astype(BF)
    lo = (ss - hi.astype(F32)).astype(BF)
    lane = lax.broadcasted_iota(I32, (256, 128), 1)
    tail = jnp.where(lane == 0, hi.astype(F32), jnp.where(lane == 1, lo.astype(F32), 0.0))
    pk[:, 896:] = tail.astype(BF)
    pk[:, :896] = (mm(xg[:, :512], go[...]) + mm(xg[:, 512:], gp[...])).astype(BF)
    for s in range(4):
        first = ((4 - s) % 4) * 64
        outs[s][...] = pk[first:first + 64, :]
    group = pos[3] // 4
    first = pl.multiple_of(lax.rem(pos[0] - group + 4, 4) * 64 + lax.rem(pos[3], 4) * 16, 16)
    xsel[...] = xr[pl.ds(first, 16), :]


def up_kernel(pos, xg, uo, up, *refs):
    outs, pk = refs[:4], refs[4]
    pk[...] = (mm(xg[:, :512], uo[...]) + mm(xg[:, 512:], up[...])).astype(BF)
    for s in range(4):
        first = ((4 - s) % 4) * 64
        outs[s][...] = pk[first:first + 64, :]


def down_kernel(pos, *refs):
    parts, down_own, down_oth, out, hid = refs[:4], refs[4], refs[5], refs[6], refs[7]
    for s in range(4):
        first = pl.multiple_of(lax.rem(pos[0] - s + 4, 4) * 64, 64)
        hid[pl.ds(first, 64), :] = parts[s][...]
    for q, w in enumerate((down_own, down_oth)):
        out[:, q * 512:(q + 1) * 512] = mm(hid[...], w[...]).astype(BF)


def split_kernel(pos, resid, mine, give):
    c = pos[2]
    for b in range(4):
        mine[b * 16:(b + 1) * 16, :] = resid[pl.ds(pl.multiple_of(b * 32 + c * 16, 16), 16), :]
        give[b * 16:(b + 1) * 16, :] = resid[pl.ds(pl.multiple_of(b * 32 + (1 - c) * 16, 16), 16), :]


def width_kernel(pos, mine, other, gain, gain_o, *outs):
    for s in range(4):
        col = pl.multiple_of(lax.rem(pos[0] + s, 4) * 512, 512)
        outs[s][:, :512] = mine[:, pl.ds(col, 512)]
        outs[s][:, 512:] = other[:, pl.ds(col, 512)]
    col = pl.multiple_of(pos[0] * 512, 512)
    outs[4][:, :512] = gain[:, pl.ds(col, 512)]
    outs[4][:, 512:] = gain_o[:, pl.ds(col, 512)]


def table_kernel(pos, sid, out):
    lane128 = lax.broadcasted_iota(I32, (32, 128), 1)
    block0 = pos[4] >> 7

    def step(t, carry):
        rows = pl.ds(pl.multiple_of(t * 32, 32), 32)
        ids = sid[rows, :]
        base = jnp.where(t >= ROWS // 64, 64, 0)
        slots = []
        for s in range(8):
            acc = jnp.full((32, 128), -1, I32)
            for i in range(8):
                j = s * 8 + i
                acc = jnp.where((ids[:, j:j + 1] & 127) == lane128, base + j, acc)
            slots.append((jnp.broadcast_to((ids[:, s * 8:s * 8 + 1] >> 7) - block0, (32, 128)), acc))
        for b in range(8):
            acc = jnp.full((32, 128), -1, I32)
            for block, slot in slots:
                acc = jnp.where(block == b, slot, acc)
            out[rows, b * 128:(b + 1) * 128] = acc.astype(jnp.int8)
        return carry

    lax.fori_loop(0, ROWS // 32, step, 0)


def chosen(rank, row, start):
    seat = lax.broadcasted_iota(I32, (SEATS, 128), 0)
    return jnp.where(rank[pl.ds(row, 1), :] == seat + start, 1.0, 0.0).astype(BF)


def pack_kernel():
    def kernel(pos, rows, rank, *outs):
        for s in range(4):
            slab = lax.rem(pos[0] + s, 4)
            for g in range(4):
                pick = chosen(rank, slab * 4 + g, pos[5])
                outs[s][g * SEATS:(g + 1) * SEATS, :] = mm(pick, rows[g * 128:(g + 1) * 128, :]).astype(BF)

    return kernel


def ids_kernel():
    def kernel(pos, hi, lo, rank, out):
        for g in range(4):
            pick = chosen(rank, pos[0] * 4 + g, pos[5])
            at = slice(g * 128, (g + 1) * 128)
            both = mm(pick, hi[at, :]) * 256.0 + mm(pick, lo[at, :])
            out[g * SEATS:(g + 1) * SEATS, :] = both.astype(I32) - 1

    return kernel


def unpack_kernel():
    def kernel(pos, p0, p1, p2, p3, rank, out, picks, vals):
        for s, part in enumerate((p0, p1, p2, p3)):
            slab = lax.rem(pos[0] - s + 4, 4)
            picks[s * SEATS:(s + 1) * SEATS, :] = chosen(rank, slab * 4 + pos[0], pos[5])
            vals[s * SEATS:(s + 1) * SEATS, :] = part[...]

        def product(n, carry):
            at = pl.ds(pl.multiple_of(n * 512, 512), 512)
            out[:, at] = lax.dot_general(
                picks[...], vals[:, at], (((0,), (0,)), ((), ())), preferred_element_type=F32
            )
            return carry

        lax.fori_loop(0, 4, product, 0)

    return kernel


def lookup(values, index):
    return jnp.take_along_axis(values, index, axis=1, mode="promise_in_bounds")


def encode_kernel(pos, p0, p1, p2, p3, enc, bias, dec_bias, sidp, out, cent, pre):
    lane128 = lax.broadcasted_iota(I32, (64, 128), 1)
    for s, part in enumerate((p0, p1, p2, p3)):
        at = pl.ds(pl.multiple_of(lax.rem(pos[0] - s + 4, 4) * 512, 512), 512)
        cent[:, at] = (part[...].astype(F32) - dec_bias[:, at]).astype(BF)

    def product(n, carry):
        cols = pl.ds(pl.multiple_of(n * 256, 256), 256)
        pre[:, cols] = mm(cent[...], enc[:, cols]) + bias[:, cols]
        return carry

    lax.fori_loop(0, 4, product, 0)

    def compress(t, carry):
        rows = pl.ds(pl.multiple_of(t * 64, 64), 64)
        rows_hi = pl.ds(pl.multiple_of(ROWS // 2 + t * 64, 64), 64)
        ids = sidp[rows, :]
        lane = ids & 127
        block = (ids >> 7) - (pos[4] >> 7)
        acc = jnp.zeros((64, 128), F32)
        for b in range(8):
            lo = lookup(pre[rows, b * 128:(b + 1) * 128], lane)
            hi = lookup(pre[rows_hi, b * 128:(b + 1) * 128], lane)
            acc = jnp.where(block == b, jnp.where(lane128 < 64, lo, hi), acc)
        out[rows, :] = acc
        return carry

    lax.fori_loop(0, ROWS // 128, compress, 0)


def decode_kernel(pos, total, table, dec, *refs):
    outs, act, dense, y = refs[:4], refs[4], refs[5], refs[6]
    act[...] = jnp.maximum(total[...], 0.0)

    def step(t, carry):
        rows = pl.ds(pl.multiple_of(t * 64, 64), 64)
        vals = act[pl.ds(pl.multiple_of(lax.rem(t, ROWS // 128) * 64, 64), 64), :]
        for b in range(8):
            idx = table[rows, b * 128:(b + 1) * 128].astype(I32)
            got = lookup(vals, jnp.maximum(idx, 0))
            dense[rows, b * 128:(b + 1) * 128] = jnp.where(idx >= 0, got, 0.0).astype(BF)
        return carry

    lax.fori_loop(0, ROWS // 64, step, 0)

    def product(g, carry):
        at = pl.ds(pl.multiple_of(g * 256, 256), 256)
        y[:, at] = mm(dense[...], dec[:, at]).astype(BF)
        return carry

    lax.fori_loop(0, 8, product, 0)
    for s in range(4):
        first = pl.multiple_of(lax.rem(pos[0] + s, 4) * SEATS, SEATS)
        outs[s][...] = y[pl.ds(first, SEATS), :]


def swap(x, axis):
    return lax.ppermute(x, axis, [(0, 1), (1, 0)])


def dp_shift(x, s):
    return lax.ppermute(x, "dp", [(i, (i + s) % 4) for i in range(4)])


def body(resid, norm_gain, gate_w, up_w, down_w, enc, enc_bias, dec, dec_bias, ids):
    d, x, c = lax.axis_index("dp"), lax.axis_index("xlo"), lax.axis_index("core")
    h, z = lax.axis_index("xhi"), lax.axis_index("z")
    tensor = h * 8 + z
    pos = jnp.stack([d, x, c, tensor, (d * 16 + tensor) * 1024, d, d, d]).astype(I32)

    wide = norm_gain.reshape(1, 2048)
    mine, give = call(split_kernel, [sds((64, 2048), BF)] * 2, 1, [], 0, 1_000_000)(pos, resid)
    other, gain_o = swap(give, "core"), swap(wide, "core")
    gate, up, down = gate_w[0], up_w[0], down_w[:, 0, :]
    gate_o, up_o, down_o = swap(gate, "core"), swap(up, "core"), swap(down, "core")
    *xw, gain = call(
        width_kernel, [sds((64, 1024), BF)] * 4 + [sds((1, 1024), F32)], 4, [], 0, 1_000_000
    )(pos, mine, other, wide, gain_o)
    xs = [xw[0]] + [dp_shift(xw[s], s) for s in range(1, 4)]

    rank = jnp.sum((ids[:, :, None] < ids[:, None, :]).astype(I32), axis=1)
    place = lax.broadcasted_iota(I32, (1, 64, 64), 1)
    sid = jnp.sum(jnp.where(rank[:, None, :] == place, ids[:, None, :], 0), axis=2)
    id_hi, id_lo = ((sid + 1) >> 8).astype(BF), ((sid + 1) & 255).astype(BF)
    slabs = ids >> 10
    uses = jnp.stack([jnp.any(slabs == a * 16 + tensor, axis=1) for a in range(4)]).reshape(16, 128)
    before = (lax.broadcasted_iota(I32, (128, 128), 0) < lax.broadcasted_iota(I32, (128, 128), 1)).astype(BF)
    rank = jnp.where(uses, mm(uses.astype(BF), before).astype(I32), -1)
    res = call(
        gate_kernel, [sds((64, 1024), BF)] * 4 + [sds((16, 1024), F32), sds((256, 1024), BF)], 7,
        [pltpu.VMEM((256, 1024), BF), pltpu.VMEM((256, 1024), F32)], 470_000_000, 3_000_000,
    )(pos, *xs, gain, gate, gate_o)
    xsel, xg = res[4], res[5]
    res_u = call(
        up_kernel, [sds((64, 896), BF)] * 4, 3, [pltpu.VMEM((256, 896), BF)], 470_000_000, 3_000_000
    )(pos, xg, up, up_o)

    def width_sum(pieces):
        tot = pieces[0].astype(F32)
        for s in range(1, 4):
            tot = tot + dp_shift(pieces[s], s).astype(F32)
        return tot + swap(tot.astype(BF), "xlo").astype(F32)

    tot_g, tot_u = width_sum(res[:4]), width_sum(res_u)
    inv = lax.rsqrt((tot_g[:, 896:897] + tot_g[:, 897:898]) / 8192 + 1e-05)
    hidden = (jax.nn.silu(tot_g[:, :896] * inv) * (tot_u * inv)).astype(BF)
    hid = [hidden] + [dp_shift(hidden, s) for s in range(1, 4)]
    terms = call(
        down_kernel, sds((256, 1024), BF), 6, [pltpu.VMEM((256, 896), BF)], 470_000_000, 3_000_000
    )(pos, *hid, down, down_o)
    terms = lax.all_to_all(terms, ("xhi", "z"), 0, 0, tiled=True)
    block_sum = jnp.sum(terms.reshape(16, 16, 1024).astype(F32), axis=0)
    rows = (xsel + block_sum).astype(BF)

    own, crossed = rows[:, :512], swap(rows[:, 512:], "core")
    rows = jnp.where(c == 0, jnp.stack([own, crossed]), jnp.stack([crossed, own])).reshape(32, 512)
    rows = jnp.broadcast_to(rows[None], (16, 32, 512)).reshape(512, 512)
    slabs_late, _ = lax.optimization_barrier((slabs, rows))
    every = lax.broadcasted_iota(I32, (1, 1, 64), 2)
    used = jnp.any(slabs_late[:, :, None] == every, axis=1)
    fullest = jnp.max(jnp.sum(used.reshape(4, 128, 64).astype(I32), axis=1))
    rows = lax.all_to_all(rows, ("xhi", "z"), 0, 0, tiled=True)

    lead = ((x == 0) & (c == 0)).astype(F32)
    bias = (enc_bias * lead).reshape(1, 1024)
    wide_bias = dec_bias.reshape(1, 2048)

    def dp_all(pieces):
        return [pieces[0]] + [dp_shift(pieces[s], s) for s in range(1, 4)]

    def sparse_round(start, pos=pos):
        pos = pos.at[5].set(start)
        packed = call(
            pack_kernel(), [sds((ROWS, 512), BF)] * 4, 2, [], 300_000_000, 2_000_000
        )(pos, rows, rank)
        parts = dp_all(packed)
        at, _ = lax.optimization_barrier((pos, packed[3]))
        seated = call(ids_kernel(), sds((ROWS, 64), I32), 3, [], 10_000_000, 200_000)(
            at, id_hi, id_lo, rank
        )
        table = call(table_kernel, sds((ROWS, 1024), jnp.int8), 1, [], 500_000_000, 10_000_000)(at, seated)
        paired = jnp.concatenate([seated[:ROWS // 2], seated[ROWS // 2:]], axis=1)
        paired, table = lax.optimization_barrier((paired, table))
        comp = call(
            encode_kernel, sds((ROWS // 2, 128), F32), 8,
            [pltpu.VMEM((ROWS, 2048), BF), pltpu.VMEM((ROWS, 1024), F32)],
            1_100_000_000, 6_000_000, limit=20,
        )(pos, *parts, enc, bias, wide_bias, paired)
        for axis in ("core", "xlo"):
            comp = comp + swap(comp.astype(BF), axis).astype(F32)
        ys = call(
            decode_kernel, [sds((SEATS, 2048), BF)] * 4, 3,
            [pltpu.VMEM((ROWS // 2, 128), F32), pltpu.VMEM((ROWS, 1024), BF), pltpu.VMEM((ROWS, 2048), BF)],
            1_100_000_000, 8_000_000, limit=20,
        )(pos, comp, table, dec)
        ys = dp_all(ys)
        return call(
            unpack_kernel(), sds((128, 2048), F32), 5,
            [pltpu.VMEM((ROWS, 128), BF), pltpu.VMEM((ROWS, 2048), BF)], 140_000_000, 2_000_000,
        )(pos, *ys, rank)

    rounds = lax.div(fullest + SEATS - 1, SEATS)
    y = lax.fori_loop(0, rounds, lambda i, v: v + sparse_round(i * SEATS), jnp.zeros((128, 2048), F32))
    y = lax.all_to_all(y.astype(BF), ("xhi", "z"), 0, 0, tiled=True)
    decoded = jnp.sum(y.reshape(16, 8, 2048).astype(F32), axis=0) + wide_bias

    rel = jnp.stack(
        dp_all([lax.dynamic_slice_in_dim(rows, lax.rem(d + s, 4) * 128 + tensor * 8, 8, 0) for s in range(4)])
    )
    kept = jnp.concatenate(
        [lax.dynamic_index_in_dim(rel, (d - g + 4) % 4, 0, keepdims=False) for g in range(4)], 1
    )
    kept_f = kept.astype(F32)
    misfit = kept_f - decoded
    sums = jnp.stack([jnp.sum(misfit * misfit, axis=1), jnp.sum(kept_f * kept_f, axis=1)])
    for axis in ("core", "xlo"):
        sums = sums + swap(sums, axis)
    return kept, decoded.astype(BF), sums[0] / (sums[1] + 1e-06)


def solution(mesh):
    fine = Mesh(mesh.devices.reshape(4, 2, 8, 2, 2), ("dp", "xhi", "z", "xlo", "core"))
    rep, tensor, slabs = ("xlo", "core"), ("xhi", "z"), ("dp", "xhi", "z")
    in_specs = (
        P("dp", rep), P(rep), P(rep, "dp", tensor), P(rep, "dp", tensor), P(tensor, rep, "dp"),
        P(rep, slabs), P(slabs), P(slabs, rep), P(rep), P(),
    )
    out_specs = (P(slabs, rep), P(slabs, rep), P(slabs))
    return jax.shard_map(body, mesh=fine, in_specs=in_specs, out_specs=out_specs, check_vma=False)
```

profile of v0, /device:TPU:1, one launch (start us, length us, event | category | flops | bytes accessed | tf_op | source)
XLA Modules:
  0.0 184.4 jit_solution(7229805523933258430)
XLA Ops:
  0.6 3.3 %collective-permute-start.13 = (bf16[512,896]{1,0:T(8,128)(2,1)}, bf16[512,896]{1,0:T(8,128)(2,1)S(1)}, u32[]{:S(2)}, u32[]{:S(2)}) collective-permute-start(bf16[512,896]{1,0:T(8,128)(2,1)} %bitcast.44), channel_id=1, source_target_pairs={{0,1},{1,0},{2,3},{3,2},{4,5},{5,4},{6,7},{7,6},{8,9},{9,8},{10,11... | collective-permute-start | bytes 2752520 | tf_op jit(solution)/shard_map/ppermute | solution.py:229
  12.5 3.3 %collective-permute-done.10.p1 = bf16[64,1024]{1,0:T(8,128)(2,1)S(1)} collective-permute-done((bf16[64,1024]{1,0:T(8,128)(2,1)S(1)}, bf16[64,1024]{1,0:T(8,128)(2,1)S(1)}, u32[]{:S(2)}, u32[]{:S(2)}) %collective-permute-start.10) | collective-permute-done | bytes 131104 | tf_op jit(solution)/shard_map/ppermute | solution.py:233
  20.8 3.4 %collective-permute-start.16 = (bf16[64,1024]{1,0:T(8,128)(2,1)S(1)}, bf16[64,1024]{1,0:T(8,128)(2,1)S(1)}, u32[]{:S(2)}, u32[]{:S(2)}) collective-permute-start(bf16[64,1024]{1,0:T(8,128)(2,1)S(1)} %get-tuple-element.234), channel_id=1, source_target_pairs={{0,192},{64,0},{128,64},{192,128},{1,193},{65,1},{129,65},{193,129... | collective-permute-start | bytes 393224 | tf_op jit(solution)/shard_map/ppermute | solution.py:233
  36.7 2.8 %collective-permute-done.19 = bf16[64,896]{1,0:T(8,128)(2,1)S(1)} collective-permute-done((bf16[64,896]{1,0:T(8,128)(2,1)S(1)}, bf16[64,896]{1,0:T(8,128)(2,1)S(1)}, u32[]{:S(2)}, u32[]{:S(2)}) %collective-permute-start.19) | collective-permute-done | bytes 114720 | tf_op jit(solution)/shard_map/ppermute | solution.py:233
  43.7 2.7 %collective-permute-start.24 = (bf16[64,896]{1,0:T(8,128)(2,1)S(1)}, bf16[64,896]{1,0:T(8,128)(2,1)S(1)}, u32[]{:S(2)}, u32[]{:S(2)}) collective-permute-start(bf16[64,896]{1,0:T(8,128)(2,1)S(1)} %multiply_convert_fusion.refs_0_), channel_id=1, source_target_pairs={{0,128},{64,192},{128,0},{192,64},{1,129},{65,193},{129,1},{193,65... | collective-permute-start | bytes 344072 | tf_op jit(solution)/shard_map/ppermute | solution.py:233
  52.7 11.5 %all-to-all-start = ((bf16[16,16,1024]{2,1,0:T(8,128)(2,1)}), bf16[16,16,1024]{2,1,0:T(8,128)(2,1)S(1)}, u32[]{:S(2)}, u32[]{:S(2)}) async-start(bf16[16,16,1024]{2,1,0:T(8,128)(2,1)} %bitcast.10), calls=%async_computation | async-start | bytes 1048576 | tf_op jit(solution)/shard_map/all_to_all | solution.py:282
  66.4 11.7 %all-to-all-done = bf16[16,16,1024]{2,1,0:T(8,128)(2,1)S(1)} async-done(((bf16[16,16,1024]{2,1,0:T(8,128)(2,1)}), bf16[16,16,1024]{2,1,0:T(8,128)(2,1)S(1)}, u32[]{:S(2)}, u32[]{:S(2)}) %all-to-all-start) | async-done | bytes 524320 | tf_op jit(solution)/shard_map/all_to_all | solution.py:282
  78.2 3.7 %collective-permute-start.27 = (bf16[16,512]{1,0:T(8,128)(2,1)S(1)}, bf16[16,512]{1,0:T(8,128)(2,1)S(1)}, u32[]{:S(2)}, u32[]{:S(2)}) collective-permute-start(bf16[16,512]{1,0:T(8,128)(2,1)S(1)} %get-tuple-element.298), channel_id=1, source_target_pairs={{0,1},{1,0},{2,3},{3,2},{4,5},{5,4},{6,7},{7,6},{8,9},{9,8},{10,11... | collective-permute-start | bytes 49160 | tf_op jit(solution)/shard_map/ppermute | solution.py:229
  85.4 4.9 %all-to-all-start.1 = ((bf16[16,32,512]{2,1,0:T(8,128)(2,1)}), bf16[16,32,512]{2,1,0:T(8,128)(2,1)}, u32[]{:S(2)}, u32[]{:S(2)}) async-start(bf16[16,32,512]{2,1,0:T(8,128)(2,1)} %broadcast_in_dim.18), calls=%async_computation.1 | async-start | bytes 1048576 | tf_op jit(solution)/shard_map/all_to_all | solution.py:293
  91.8 14.5 %all-to-all-done.1 = bf16[16,32,512]{2,1,0:T(8,128)(2,1)} async-done(((bf16[16,32,512]{2,1,0:T(8,128)(2,1)}), bf16[16,32,512]{2,1,0:T(8,128)(2,1)}, u32[]{:S(2)}, u32[]{:S(2)}) %all-to-all-start.1) | async-done | bytes 524320 | tf_op jit(solution)/shard_map/all_to_all | solution.py:293
  106.4 48.8 %while.14 = (s32[]{:T(128)}, f32[128,2048]{1,0:T(8,128)S(1)}, s32[]{:T(128)}, s32[8]{0:T(128)S(1)}, bf16[512,512]{1,0:T(8,128)(2,1)}, /*index=5*/s32[16,128]{1,0...) while((s32[]{:T(128)}, f32[128,2048]{1,0:T(8,128)S(1)}, ...), condition=%wide.region_11.12_spmd, body=%wide.region_10.11_spmd.sunk | while | flops 3150409472 | bytes 55365264 | solution.py:334
  108.4 4.3 %collective-permute-start.1 = (bf16[256,512]{1,0:T(8,128)(2,1)S(1)}, bf16[256,512]{1,0:T(8,128)(2,1)S(1)}, u32[]{:S(2)}, u32[]{:S(2)}) collective-permute-start(bf16[256,512]{1,0:T(8,128)(2,1)S(1)} %get-tuple-element.388), channel_id=1, source_target_pairs={{0,128},{64,192},{128,0},{192,64},{1,129},{65,193},{129,1},{193,65... | collective-permute-start | bytes 786440 | tf_op jit(solution)/shard_map/while/body/ppermute | solution.py:233
  113.5 4.5 %body.28.table = s8[256,1024]{1,0:T(32,128)(4,1)S(1)} custom-call(s32[8]{0:T(128)S(1)} %constant_dynamic-update-slice_fusion.2.pos, s32[256,64]{1,0:T(8,128)S(1)} %body.27.sid), custom_call_target="tpu_custom_call" | custom-call | flops 500000000 | bytes 10000000 | tf_op jit(solution)/shard_map/while/body/pallas_call | solution.py:312
  118.1 4.6 %collective-permute-done.1.p2 = bf16[256,512]{1,0:T(8,128)(2,1)S(1)} collective-permute-done((bf16[256,512]{1,0:T(8,128)(2,1)S(1)}, bf16[256,512]{1,0:T(8,128)(2,1)S(1)}, u32[]{:S(2)}, u32[]{:S(2)}) %collective-permute-start.1) | collective-permute-done | bytes 262176 | tf_op jit(solution)/shard_map/while/body/ppermute | solution.py:233
  123.5 5.1 %body.29 = f32[128,128]{1,0:T(8,128)S(1)} custom-call(s32[8]{0:T(128)S(1)} %constant_dynamic-update-slice_fusion.2.pos, bf16[256,512]{1,0:T(8,128)(2,1)S(1)} %get-tuple-element.386.p0, bf16[256,512]{1,0:T(8,128)(2,1)S(1)} %collective-permute-done.p1, bf16[256,512]{1,0:T(8,128)(2,1)S(1)} %collective-permute-done.1.p2, ...), custom_call_target="tpu_custom_call" | custom-call | flops 1100000000 | bytes 6000000 | tf_op jit(solution)/shard_map/while/body/pallas_call | solution.py:315
  134.6 4.2 %body.30 = (bf16[64,2048]{1,0:T(8,128)(2,1)S(1)}, bf16[64,2048]{1,0:T(8,128)(2,1)S(1)}, bf16[64,2048]{1,0:T(8,128)(2,1)S(1)}, bf16[64,2048]{1,0:T(8,128)(2,1)S(1)}) custom-call(s32[8]{0:T(128)S(1)} %constant_dynamic-update-slice_fusion.2.pos, f32[128,128]{1,0:T(8,128)S(1)} %convert_add_fusion.6.total, s8[256,1024]{1,0:T(32,128)(4,1)S(1)} %body.28.table, ...), custom_call_target="tpu_custom_call" | custom-call | flops 1100000000 | bytes 8000000 | tf_op jit(solution)/shard_map/while/body/pallas_call | solution.py:322
  138.8 3.0 %collective-permute-start.6 = (bf16[64,2048]{1,0:T(8,128)(2,1)S(1)}, bf16[64,2048]{1,0:T(8,128)(2,1)S(1)}, u32[]{:S(2)}, u32[]{:S(2)}) collective-permute-start(bf16[64,2048]{1,0:T(8,128)(2,1)S(1)} %get-tuple-element.397), channel_id=1, source_target_pairs={{0,128},{64,192},{128,0},{192,64},{1,129},{65,193},{129,1},{193,65... | collective-permute-start | bytes 786440 | tf_op jit(solution)/shard_map/while/body/ppermute | solution.py:233
  141.9 4.4 %collective-permute-done.5.p1 = bf16[64,2048]{1,0:T(8,128)(2,1)S(1)} collective-permute-done((bf16[64,2048]{1,0:T(8,128)(2,1)S(1)}, bf16[64,2048]{1,0:T(8,128)(2,1)S(1)}, u32[]{:S(2)}, u32[]{:S(2)}) %collective-permute-start.5) | collective-permute-done | bytes 262176 | tf_op jit(solution)/shard_map/while/body/ppermute | solution.py:233
  146.3 6.0 %collective-permute-done.6.p2 = bf16[64,2048]{1,0:T(8,128)(2,1)S(1)} collective-permute-done((bf16[64,2048]{1,0:T(8,128)(2,1)S(1)}, bf16[64,2048]{1,0:T(8,128)(2,1)S(1)}, u32[]{:S(2)}, u32[]{:S(2)}) %collective-permute-start.6) | collective-permute-done | bytes 262176 | tf_op jit(solution)/shard_map/while/body/ppermute | solution.py:233
  156.1 6.0 %all-to-all-start.2 = ((bf16[16,8,2048]{2,1,0:T(8,128)(2,1)}), bf16[16,8,2048]{2,1,0:T(8,128)(2,1)S(1)}, u32[]{:S(2)}, u32[]{:S(2)}) async-start(bf16[16,8,2048]{2,1,0:T(8,128)(2,1)} %convert_bitcast_fusion), calls=%async_computation.2 | async-start | bytes 1048576 | tf_op jit(solution)/shard_map/all_to_all | solution.py:335
  162.8 3.4 %collective-permute-start.30 = (bf16[8,512]{1,0:T(8,128)(2,1)S(1)}, bf16[8,512]{1,0:T(8,128)(2,1)S(1)}, u32[]{:S(2)}, u32[]{:S(2)}) collective-permute-start(bf16[8,512]{1,0:T(8,128)(2,1)S(1)} %get-tuple-element.287), channel_id=1, source_target_pairs={{0,192},{64,0},{128,64},{192,128},{1,193},{65,1},{129,65},{193,129... | collective-permute-start | bytes 24584 | tf_op jit(solution)/shard_map/ppermute | solution.py:233
  167.1 3.2 %collective-permute-done.29 = bf16[8,512]{1,0:T(8,128)(2,1)S(1)} collective-permute-done((bf16[8,512]{1,0:T(8,128)(2,1)S(1)}, bf16[8,512]{1,0:T(8,128)(2,1)S(1)}, u32[]{:S(2)}, u32[]{:S(2)}) %collective-permute-start.29) | collective-permute-done | bytes 8224 | tf_op jit(solution)/shard_map/ppermute | solution.py:233
  170.3 6.2 %all-to-all-done.2 = bf16[16,8,2048]{2,1,0:T(8,128)(2,1)S(1)} async-done(((bf16[16,8,2048]{2,1,0:T(8,128)(2,1)}), bf16[16,8,2048]{2,1,0:T(8,128)(2,1)S(1)}, u32[]{:S(2)}, u32[]{:S(2)}) %all-to-all-start.2) | async-done | bytes 524320 | tf_op jit(solution)/shard_map/all_to_all | solution.py:335
  177.4 3.2 %collective-permute-start.31 = (f32[2,8]{1,0:T(2,128)S(1)}, f32[2,8]{1,0:T(2,128)S(1)}, u32[]{:S(2)}, u32[]{:S(2)}) collective-permute-start(f32[2,8]{1,0:T(2,128)S(1)} %pad_maximum_fusion.2), channel_id=1, source_target_pairs={{0,1},{1,0},{2,3},{3,2},{4,5},{5,4},{6,7},{7,6},{8,9},{9,8},{10,11... | collective-permute-start | bytes 200 | tf_op jit(solution)/shard_map/ppermute | solution.py:229
  (128 shorter events, 62.5 us)
Async XLA Ops:
  0.6 17.7 %collective-permute-start.13 = (bf16[512,896]{1,0:T(8,128)(2,1)}, bf16[512,896]{1,0:T(8,128)(2,1)S(1)}, u32[]{:S(2)}, u32[]{:S(2)}) collective-permute-start(bf16[512,896]{1,0:T(8,128)(2,1)} %bitcast.44), channel_id=1, source_target_pairs={{0,1},{1,0},{2,3},{3,2},{4,5},{5,4},{6,7},{7,6},{8,9},{9,8},{10,11... | collective-permute-start | bytes 2752520 | tf_op jit(solution)/shard_map/ppermute | solution.py:229
  4.0 21.9 %collective-permute-start.18 = (bf16[512,896]{1,0:T(8,128)(2,1)}, bf16[512,896]{1,0:T(8,128)(2,1)S(1)}, u32[]{:S(2)}, u32[]{:S(2)}) collective-permute-start(bf16[512,896]{1,0:T(8,128)(2,1)} %bitcast.42), channel_id=1, source_target_pairs={{0,1},{1,0},{2,3},{3,2},{4,5},{5,4},{6,7},{7,6},{8,9},{9,8},{10,11... | collective-permute-start | bytes 2752520 | tf_op jit(solution)/shard_map/ppermute | solution.py:229
  9.1 6.6 %collective-permute-start.10 = (bf16[64,1024]{1,0:T(8,128)(2,1)S(1)}, bf16[64,1024]{1,0:T(8,128)(2,1)S(1)}, u32[]{:S(2)}, u32[]{:S(2)}) collective-permute-start(bf16[64,1024]{1,0:T(8,128)(2,1)S(1)} %get-tuple-element.226), channel_id=1, source_target_pairs={{0,64},{64,128},{128,192},{192,0},{1,65},{65,129},{129,193},{193,1... | collective-permute-start | bytes 393224 | tf_op jit(solution)/shard_map/ppermute | solution.py:233
  9.2 8.4 %collective-permute-start.11 = (bf16[64,1024]{1,0:T(8,128)(2,1)S(1)}, bf16[64,1024]{1,0:T(8,128)(2,1)S(1)}, u32[]{:S(2)}, u32[]{:S(2)}) collective-permute-start(bf16[64,1024]{1,0:T(8,128)(2,1)S(1)} %get-tuple-element.227), channel_id=1, source_target_pairs={{0,128},{64,192},{128,0},{192,64},{1,129},{65,193},{129,1},{193,65... | collective-permute-start | bytes 393224 | tf_op jit(solution)/shard_map/ppermute | solution.py:233
  11.4 6.9 %collective-permute-start.12 = (bf16[64,1024]{1,0:T(8,128)(2,1)S(1)}, bf16[64,1024]{1,0:T(8,128)(2,1)S(1)}, u32[]{:S(2)}, u32[]{:S(2)}) collective-permute-start(bf16[64,1024]{1,0:T(8,128)(2,1)S(1)} %get-tuple-element.228), channel_id=1, source_target_pairs={{0,192},{64,0},{128,64},{192,128},{1,193},{65,1},{129,65},{193,129... | collective-permute-start | bytes 393224 | tf_op jit(solution)/shard_map/ppermute | solution.py:233
  20.8 9.9 %collective-permute-start.16 = (bf16[64,1024]{1,0:T(8,128)(2,1)S(1)}, bf16[64,1024]{1,0:T(8,128)(2,1)S(1)}, u32[]{:S(2)}, u32[]{:S(2)}) collective-permute-start(bf16[64,1024]{1,0:T(8,128)(2,1)S(1)} %get-tuple-element.234), channel_id=1, source_target_pairs={{0,192},{64,0},{128,64},{192,128},{1,193},{65,1},{129,65},{193,129... | collective-permute-start | bytes 393224 | tf_op jit(solution)/shard_map/ppermute | solution.py:233
  24.2 8.3 %collective-permute-start.15 = (bf16[64,1024]{1,0:T(8,128)(2,1)S(1)}, bf16[64,1024]{1,0:T(8,128)(2,1)S(1)}, u32[]{:S(2)}, u32[]{:S(2)}) collective-permute-start(bf16[64,1024]{1,0:T(8,128)(2,1)S(1)} %get-tuple-element.233), channel_id=1, source_target_pairs={{0,128},{64,192},{128,0},{192,64},{1,129},{65,193},{129,1},{193,65... | collective-permute-start | bytes 393224 | tf_op jit(solution)/shard_map/ppermute | solution.py:233
  24.2 9.5 %collective-permute-start.14 = (bf16[64,1024]{1,0:T(8,128)(2,1)S(1)}, bf16[64,1024]{1,0:T(8,128)(2,1)S(1)}, u32[]{:S(2)}, u32[]{:S(2)}) collective-permute-start(bf16[64,1024]{1,0:T(8,128)(2,1)S(1)} %get-tuple-element.232), channel_id=1, source_target_pairs={{0,64},{64,128},{128,192},{192,0},{1,65},{65,129},{129,193},{193,1... | collective-permute-start | bytes 393224 | tf_op jit(solution)/shard_map/ppermute | solution.py:233
  24.8 23.5 %collective-permute-start.26 = (bf16[896,512]{1,0:T(8,128)(2,1)}, bf16[896,512]{1,0:T(8,128)(2,1)S(1)}, u32[]{:S(2)}, u32[]{:S(2)}) collective-permute-start(bf16[896,512]{1,0:T(8,128)(2,1)} %bitcast.46), channel_id=1, source_target_pairs={{0,1},{1,0},{2,3},{3,2},{4,5},{5,4},{6,7},{7,6},{8,9},{9,8},{10,11... | collective-permute-start | bytes 2752520 | tf_op jit(solution)/shard_map/ppermute | solution.py:229
  28.4 5.9 %collective-permute-start.21 = (bf16[64,896]{1,0:T(8,128)(2,1)S(1)}, bf16[64,896]{1,0:T(8,128)(2,1)S(1)}, u32[]{:S(2)}, u32[]{:S(2)}) collective-permute-start(bf16[64,896]{1,0:T(8,128)(2,1)S(1)} %get-tuple-element.239), channel_id=1, source_target_pairs={{0,192},{64,0},{128,64},{192,128},{1,193},{65,1},{129,65},{193,129... | collective-permute-start | bytes 344072 | tf_op jit(solution)/shard_map/ppermute | solution.py:233
  30.7 6.0 %collective-permute-start.20 = (bf16[64,896]{1,0:T(8,128)(2,1)S(1)}, bf16[64,896]{1,0:T(8,128)(2,1)S(1)}, u32[]{:S(2)}, u32[]{:S(2)}) collective-permute-start(bf16[64,896]{1,0:T(8,128)(2,1)S(1)} %get-tuple-element.238), channel_id=1, source_target_pairs={{0,128},{64,192},{128,0},{192,64},{1,129},{65,193},{129,1},{193,65... | collective-permute-start | bytes 344072 | tf_op jit(solution)/shard_map/ppermute | solution.py:233
  32.5 6.9 %collective-permute-start.19 = (bf16[64,896]{1,0:T(8,128)(2,1)S(1)}, bf16[64,896]{1,0:T(8,128)(2,1)S(1)}, u32[]{:S(2)}, u32[]{:S(2)}) collective-permute-start(bf16[64,896]{1,0:T(8,128)(2,1)S(1)} %get-tuple-element.237), channel_id=1, source_target_pairs={{0,64},{64,128},{128,192},{192,0},{1,65},{65,129},{129,193},{193,1... | collective-permute-start | bytes 344072 | tf_op jit(solution)/shard_map/ppermute | solution.py:233
  33.7 6.7 %collective-permute-start.17 = (bf16[64,1024]{1,0:T(8,128)(2,1)S(1)}, bf16[64,1024]{1,0:T(8,128)(2,1)S(1)}, u32[]{:S(2)}, u32[]{:S(2)}) collective-permute-start(bf16[64,1024]{1,0:T(8,128)(2,1)S(1)} %fusion.3), channel_id=1, source_target_pairs={{0,2},{2,0},{1,3},{3,1},{4,6},{6,4},{5,7},{7,5},{8,10},{10,8},{9,1... | collective-permute-start | bytes 393224 | tf_op jit(solution)/shard_map/ppermute | solution.py:229
  43.7 6.8 %collective-permute-start.24 = (bf16[64,896]{1,0:T(8,128)(2,1)S(1)}, bf16[64,896]{1,0:T(8,128)(2,1)S(1)}, u32[]{:S(2)}, u32[]{:S(2)}) collective-permute-start(bf16[64,896]{1,0:T(8,128)(2,1)S(1)} %multiply_convert_fusion.refs_0_), channel_id=1, source_target_pairs={{0,128},{64,192},{128,0},{192,64},{1,129},{65,193},{129,1},{193,65... | collective-permute-start | bytes 344072 | tf_op jit(solution)/shard_map/ppermute | solution.py:233
  52.7 25.4 %all-to-all-start = ((bf16[16,16,1024]{2,1,0:T(8,128)(2,1)}), bf16[16,16,1024]{2,1,0:T(8,128)(2,1)S(1)}, u32[]{:S(2)}, u32[]{:S(2)}) async-start(bf16[16,16,1024]{2,1,0:T(8,128)(2,1)} %bitcast.10), calls=%async_computation | async-start | bytes 1048576 | tf_op jit(solution)/shard_map/all_to_all | solution.py:282
  78.2 6.3 %collective-permute-start.27 = (bf16[16,512]{1,0:T(8,128)(2,1)S(1)}, bf16[16,512]{1,0:T(8,128)(2,1)S(1)}, u32[]{:S(2)}, u32[]{:S(2)}) collective-permute-start(bf16[16,512]{1,0:T(8,128)(2,1)S(1)} %get-tuple-element.298), channel_id=1, source_target_pairs={{0,1},{1,0},{2,3},{3,2},{4,5},{5,4},{6,7},{7,6},{8,9},{9,8},{10,11... | collective-permute-start | bytes 49160 | tf_op jit(solution)/shard_map/ppermute | solution.py:229
  85.4 20.9 %all-to-all-start.1 = ((bf16[16,32,512]{2,1,0:T(8,128)(2,1)}), bf16[16,32,512]{2,1,0:T(8,128)(2,1)}, u32[]{:S(2)}, u32[]{:S(2)}) async-start(bf16[16,32,512]{2,1,0:T(8,128)(2,1)} %broadcast_in_dim.18), calls=%async_computation.1 | async-start | bytes 1048576 | tf_op jit(solution)/shard_map/all_to_all | solution.py:293
  108.1 10.0 %collective-permute-start = (bf16[256,512]{1,0:T(8,128)(2,1)S(1)}, bf16[256,512]{1,0:T(8,128)(2,1)S(1)}, u32[]{:S(2)}, u32[]{:S(2)}) collective-permute-start(bf16[256,512]{1,0:T(8,128)(2,1)S(1)} %get-tuple-element.387), channel_id=1, source_target_pairs={{0,64},{64,128},{128,192},{192,0},{1,65},{65,129},{129,193},{193,1... | collective-permute-start | bytes 786440 | tf_op jit(solution)/shard_map/while/body/ppermute | solution.py:233
  108.4 14.4 %collective-permute-start.1 = (bf16[256,512]{1,0:T(8,128)(2,1)S(1)}, bf16[256,512]{1,0:T(8,128)(2,1)S(1)}, u32[]{:S(2)}, u32[]{:S(2)}) collective-permute-start(bf16[256,512]{1,0:T(8,128)(2,1)S(1)} %get-tuple-element.388), channel_id=1, source_target_pairs={{0,128},{64,192},{128,0},{192,64},{1,129},{65,193},{129,1},{193,65... | collective-permute-start | bytes 786440 | tf_op jit(solution)/shard_map/while/body/ppermute | solution.py:233
  112.8 10.8 %collective-permute-start.2 = (bf16[256,512]{1,0:T(8,128)(2,1)S(1)}, bf16[256,512]{1,0:T(8,128)(2,1)S(1)}, u32[]{:S(2)}, u32[]{:S(2)}) collective-permute-start(bf16[256,512]{1,0:T(8,128)(2,1)S(1)} %get-tuple-element.389), channel_id=1, source_target_pairs={{0,192},{64,0},{128,64},{192,128},{1,193},{65,1},{129,65},{193,129... | collective-permute-start | bytes 786440 | tf_op jit(solution)/shard_map/while/body/ppermute | solution.py:233
  138.8 7.6 %collective-permute-start.5 = (bf16[64,2048]{1,0:T(8,128)(2,1)S(1)}, bf16[64,2048]{1,0:T(8,128)(2,1)S(1)}, u32[]{:S(2)}, u32[]{:S(2)}) collective-permute-start(bf16[64,2048]{1,0:T(8,128)(2,1)S(1)} %get-tuple-element.396), channel_id=1, source_target_pairs={{0,64},{64,128},{128,192},{192,0},{1,65},{65,129},{129,193},{193,1... | collective-permute-start | bytes 786440 | tf_op jit(solution)/shard_map/while/body/ppermute | solution.py:233
  138.8 13.5 %collective-permute-start.6 = (bf16[64,2048]{1,0:T(8,128)(2,1)S(1)}, bf16[64,2048]{1,0:T(8,128)(2,1)S(1)}, u32[]{:S(2)}, u32[]{:S(2)}) collective-permute-start(bf16[64,2048]{1,0:T(8,128)(2,1)S(1)} %get-tuple-element.397), channel_id=1, source_target_pairs={{0,128},{64,192},{128,0},{192,64},{1,129},{65,193},{129,1},{193,65... | collective-permute-start | bytes 786440 | tf_op jit(solution)/shard_map/while/body/ppermute | solution.py:233
  141.9 11.6 %collective-permute-start.7 = (bf16[64,2048]{1,0:T(8,128)(2,1)S(1)}, bf16[64,2048]{1,0:T(8,128)(2,1)S(1)}, u32[]{:S(2)}, u32[]{:S(2)}) collective-permute-start(bf16[64,2048]{1,0:T(8,128)(2,1)S(1)} %get-tuple-element.398), channel_id=1, source_target_pairs={{0,192},{64,0},{128,64},{192,128},{1,193},{65,1},{129,65},{193,129... | collective-permute-start | bytes 786440 | tf_op jit(solution)/shard_map/while/body/ppermute | solution.py:233
  156.1 20.4 %all-to-all-start.2 = ((bf16[16,8,2048]{2,1,0:T(8,128)(2,1)}), bf16[16,8,2048]{2,1,0:T(8,128)(2,1)S(1)}, u32[]{:S(2)}, u32[]{:S(2)}) async-start(bf16[16,8,2048]{2,1,0:T(8,128)(2,1)} %convert_bitcast_fusion), calls=%async_computation.2 | async-start | bytes 1048576 | tf_op jit(solution)/shard_map/all_to_all | solution.py:335
  (21 other events, 251.8 us)
where the time goes:
time: 186 us; the launch traced here: 184 us
  waiting for transfers between devices  76.8 us (41%)
  starting transfers between devices  67.7 us (36%)
  Pallas kernels  23.2 us (12%)
  other arithmetic  8.34 us (4%)
  local copies, waits for them, and re-layouts  6.29 us (3%)
    ppermute x21, waiting for transfers between devices, dp_shift(): return lax.ppermute(x, 'dp', [(i, (i + s) % 4) for i in range(4)])  34.1 us
    ppermute x21, starting transfers between devices, dp_shift(): return lax.ppermute(x, 'dp', [(i, (i + s) % 4) for i in range(4)])  29.4 us
    ppermute x12, starting transfers between devices, swap(): return lax.ppermute(x, axis, [(0, 1), (1, 0)])  16 us
    all_to_all x1, waiting for transfers between devices, body(): rows = lax.all_to_all(rows, ('xhi', 'z'), 0, 0, tiled=True)  14.5 us
    all_to_all x1, waiting for transfers between devices, body(): terms = lax.all_to_all(terms, ('xhi', 'z'), 0, 0, tiled=True)  11.7 us
    all_to_all x1, starting transfers between devices, body(): terms = lax.all_to_all(terms, ('xhi', 'z'), 0, 0, tiled=True)  11.5 us
    ppermute x12, waiting for transfers between devices, swap(): return lax.ppermute(x, axis, [(0, 1), (1, 0)])  10.3 us
    all_to_all x1, waiting for transfers between devices, body(): y = lax.all_to_all(y.astype(BF), ('xhi', 'z'), 0, 0, tiled=True)  6.19 us
  transfers between devices with their start and end apart: 36, of which 25 were waited for; matrix products, arithmetic and copies ran while one was open for 4% of the time, Pallas kernels for 5%

commit v1 on v0

--- a/solution.py
+++ b/solution.py
@@ -279,17 +279,18 @@
     terms = call(
         down_kernel, sds((256, 1024), BF), 6, [pltpu.VMEM((256, 896), BF)], 470_000_000, 3_000_000
     )(pos, *hid, down, down_o)
+    slabs_late, _ = lax.optimization_barrier((slabs, terms))
+    every = lax.broadcasted_iota(I32, (1, 1, 64), 2)
+    used = jnp.any(slabs_late[:, :, None] == every, axis=1)
+    fullest = jnp.max(jnp.sum(used.reshape(4, 128, 64).astype(I32), axis=1))
     terms = lax.all_to_all(terms, ("xhi", "z"), 0, 0, tiled=True)
+    terms, fullest = lax.optimization_barrier((terms, fullest))
     block_sum = jnp.sum(terms.reshape(16, 16, 1024).astype(F32), axis=0)
     rows = (xsel + block_sum).astype(BF)
 
     own, crossed = rows[:, :512], swap(rows[:, 512:], "core")
     rows = jnp.where(c == 0, jnp.stack([own, crossed]), jnp.stack([crossed, own])).reshape(32, 512)
     rows = jnp.broadcast_to(rows[None], (16, 32, 512)).reshape(512, 512)
-    slabs_late, _ = lax.optimization_barrier((slabs, rows))
-    every = lax.broadcasted_iota(I32, (1, 1, 64), 2)
-    used = jnp.any(slabs_late[:, :, None] == every, axis=1)
-    fullest = jnp.max(jnp.sum(used.reshape(4, 128, 64).astype(I32), axis=1))
     rows = lax.all_to_all(rows, ("xhi", "z"), 0, 0, tiled=True)
 
     lead = ((x == 0) & (c == 0)).astype(F32)

time: 186 us -> 184 us (0.989)
  waiting for transfers between devices: 76.8 us -> 73.3 us
    all_to_all x1, waiting for transfers between devices: 11.7 us -> 9.87 us  [body(): terms = lax.all_to_all(terms, ('xhi', 'z'), 0, 0, tiled=True)]
  transfers between devices with their start and end apart: 36 -> 36, of which waited for: 25 -> 26; matrix products, arithmetic and copies ran while one was open for 4% -> 4% of each run, Pallas kernels for 5% -> 5%
where the time goes in v1:
time: 184 us; the launch traced here: 183 us
  waiting for transfers between devices  73.3 us (40%)
  starting transfers between devices  69.4 us (38%)
  Pallas kernels  23.2 us (13%)
  other arithmetic  8.34 us (5%)
  local copies, waits for them, and re-layouts  6.29 us (3%)
    ppermute x21, waiting for transfers between devices, dp_shift(): return lax.ppermute(x, 'dp', [(i, (i + s) % 4) for i in range(4)])  33.2 us
    ppermute x21, starting transfers between devices, dp_shift(): return lax.ppermute(x, 'dp', [(i, (i + s) % 4) for i in range(4)])  29.4 us
    ppermute x12, starting transfers between devices, swap(): return lax.ppermute(x, axis, [(0, 1), (1, 0)])  16.9 us
    all_to_all x1, waiting for transfers between devices, body(): rows = lax.all_to_all(rows, ('xhi', 'z'), 0, 0, tiled=True)  13 us
    all_to_all x1, starting transfers between devices, body(): terms = lax.all_to_all(terms, ('xhi', 'z'), 0, 0, tiled=True)  11.5 us
    ppermute x12, waiting for transfers between devices, swap(): return lax.ppermute(x, axis, [(0, 1), (1, 0)])  11 us
    all_to_all x1, waiting for transfers between devices, body(): terms = lax.all_to_all(terms, ('xhi', 'z'), 0, 0, tiled=True)  9.87 us
    all_to_all x1, starting transfers between devices, body(): y = lax.all_to_all(y.astype(BF), ('xhi', 'z'), 0, 0, tiled=True)  6.71 us
  transfers between devices with their start and end apart: 36, of which 26 were waited for; matrix products, arithmetic and copies ran while one was open for 4% of the time, Pallas kernels for 5%

profile of v1, /device:TPU:1, one launch (start us, length us, event | category | flops | bytes accessed | tf_op | source)
XLA Modules:
  0.0 182.6 jit_solution(16350717499762588905)
XLA Ops:
  0.6 3.3 %collective-permute-start.13 = (bf16[512,896]{1,0:T(8,128)(2,1)}, bf16[512,896]{1,0:T(8,128)(2,1)S(1)}, u32[]{:S(2)}, u32[]{:S(2)}) collective-permute-start(bf16[512,896]{1,0:T(8,128)(2,1)} %bitcast.47), channel_id=1, source_target_pairs={{0,1},{1,0},{2,3},{3,2},{4,5},{5,4},{6,7},{7,6},{8,9},{9,8},{10,11... | collective-permute-start | bytes 2752520 | tf_op jit(solution)/shard_map/ppermute | solution.py:229
  12.5 3.3 %collective-permute-done.10.p1 = bf16[64,1024]{1,0:T(8,128)(2,1)S(1)} collective-permute-done((bf16[64,1024]{1,0:T(8,128)(2,1)S(1)}, bf16[64,1024]{1,0:T(8,128)(2,1)S(1)}, u32[]{:S(2)}, u32[]{:S(2)}) %collective-permute-start.10) | collective-permute-done | bytes 131104 | tf_op jit(solution)/shard_map/ppermute | solution.py:233
  20.8 3.4 %collective-permute-start.16 = (bf16[64,1024]{1,0:T(8,128)(2,1)S(1)}, bf16[64,1024]{1,0:T(8,128)(2,1)S(1)}, u32[]{:S(2)}, u32[]{:S(2)}) collective-permute-start(bf16[64,1024]{1,0:T(8,128)(2,1)S(1)} %get-tuple-element.237), channel_id=1, source_target_pairs={{0,192},{64,0},{128,64},{192,128},{1,193},{65,1},{129,65},{193,129... | collective-permute-start | bytes 393224 | tf_op jit(solution)/shard_map/ppermute | solution.py:233
  36.7 2.8 %collective-permute-done.19 = bf16[64,896]{1,0:T(8,128)(2,1)S(1)} collective-permute-done((bf16[64,896]{1,0:T(8,128)(2,1)S(1)}, bf16[64,896]{1,0:T(8,128)(2,1)S(1)}, u32[]{:S(2)}, u32[]{:S(2)}) %collective-permute-start.19) | collective-permute-done | bytes 114720 | tf_op jit(solution)/shard_map/ppermute | solution.py:233
  52.7 11.5 %all-to-all-start = ((bf16[16,16,1024]{2,1,0:T(8,128)(2,1)}), bf16[16,16,1024]{2,1,0:T(8,128)(2,1)S(1)}, u32[]{:S(2)}, u32[]{:S(2)}) async-start(bf16[16,16,1024]{2,1,0:T(8,128)(2,1)} %bitcast.10), calls=%async_computation | async-start | bytes 1048576 | tf_op jit(solution)/shard_map/all_to_all | solution.py:286
  68.2 9.9 %all-to-all-done = bf16[16,16,1024]{2,1,0:T(8,128)(2,1)S(1)} async-done(((bf16[16,16,1024]{2,1,0:T(8,128)(2,1)}), bf16[16,16,1024]{2,1,0:T(8,128)(2,1)S(1)}, u32[]{:S(2)}, u32[]{:S(2)}) %all-to-all-start) | async-done | bytes 524320 | tf_op jit(solution)/shard_map/all_to_all | solution.py:286
  78.2 3.7 %collective-permute-start.27 = (bf16[16,512]{1,0:T(8,128)(2,1)S(1)}, bf16[16,512]{1,0:T(8,128)(2,1)S(1)}, u32[]{:S(2)}, u32[]{:S(2)}) collective-permute-start(bf16[16,512]{1,0:T(8,128)(2,1)S(1)} %get-tuple-element.304), channel_id=1, source_target_pairs={{0,1},{1,0},{2,3},{3,2},{4,5},{5,4},{6,7},{7,6},{8,9},{9,8},{10,11... | collective-permute-start | bytes 49160 | tf_op jit(solution)/shard_map/ppermute | solution.py:229
  83.6 4.9 %all-to-all-start.1 = ((bf16[16,32,512]{2,1,0:T(8,128)(2,1)}), bf16[16,32,512]{2,1,0:T(8,128)(2,1)}, u32[]{:S(2)}, u32[]{:S(2)}) async-start(bf16[16,32,512]{2,1,0:T(8,128)(2,1)} %broadcast_in_dim.18), calls=%async_computation.1 | async-start | bytes 1048576 | tf_op jit(solution)/shard_map/all_to_all | solution.py:294
  90.7 13.0 %all-to-all-done.1 = bf16[16,32,512]{2,1,0:T(8,128)(2,1)} async-done(((bf16[16,32,512]{2,1,0:T(8,128)(2,1)}), bf16[16,32,512]{2,1,0:T(8,128)(2,1)}, u32[]{:S(2)}, u32[]{:S(2)}) %all-to-all-start.1) | async-done | bytes 524320 | tf_op jit(solution)/shard_map/all_to_all | solution.py:294
  103.8 48.8 %while.14 = (s32[]{:T(128)}, f32[128,2048]{1,0:T(8,128)S(1)}, s32[]{:T(128)}, s32[8]{0:T(128)S(1)}, bf16[512,512]{1,0:T(8,128)(2,1)}, /*index=5*/s32[16,128]{1,0...) while((s32[]{:T(128)}, f32[128,2048]{1,0:T(8,128)S(1)}, ...), condition=%wide.region_11.12_spmd, body=%wide.region_10.11_spmd.sunk | while | flops 3150409472 | bytes 55365264 | solution.py:335
  105.9 4.3 %collective-permute-start.1 = (bf16[256,512]{1,0:T(8,128)(2,1)S(1)}, bf16[256,512]{1,0:T(8,128)(2,1)S(1)}, u32[]{:S(2)}, u32[]{:S(2)}) collective-permute-start(bf16[256,512]{1,0:T(8,128)(2,1)S(1)} %get-tuple-element.394), channel_id=1, source_target_pairs={{0,128},{64,192},{128,0},{192,64},{1,129},{65,193},{129,1},{193,65... | collective-permute-start | bytes 786440 | tf_op jit(solution)/shard_map/while/body/ppermute | solution.py:233
  111.0 4.5 %body.28.table = s8[256,1024]{1,0:T(32,128)(4,1)S(1)} custom-call(s32[8]{0:T(128)S(1)} %constant_dynamic-update-slice_fusion.2.pos, s32[256,64]{1,0:T(8,128)S(1)} %body.27.sid), custom_call_target="tpu_custom_call" | custom-call | flops 500000000 | bytes 10000000 | tf_op jit(solution)/shard_map/while/body/pallas_call | solution.py:313
  115.6 3.5 %collective-permute-done.1.p2 = bf16[256,512]{1,0:T(8,128)(2,1)S(1)} collective-permute-done((bf16[256,512]{1,0:T(8,128)(2,1)S(1)}, bf16[256,512]{1,0:T(8,128)(2,1)S(1)}, u32[]{:S(2)}, u32[]{:S(2)}) %collective-permute-start.1) | collective-permute-done | bytes 262176 | tf_op jit(solution)/shard_map/while/body/ppermute | solution.py:233
  120.1 5.1 %body.29 = f32[128,128]{1,0:T(8,128)S(1)} custom-call(s32[8]{0:T(128)S(1)} %constant_dynamic-update-slice_fusion.2.pos, bf16[256,512]{1,0:T(8,128)(2,1)S(1)} %get-tuple-element.392.p0, bf16[256,512]{1,0:T(8,128)(2,1)S(1)} %collective-permute-done.p1, bf16[256,512]{1,0:T(8,128)(2,1)S(1)} %collective-permute-done.1.p2, ...), custom_call_target="tpu_custom_call" | custom-call | flops 1100000000 | bytes 6000000 | tf_op jit(solution)/shard_map/while/body/pallas_call | solution.py:316
  125.2 3.1 %collective-permute-start.3 = (bf16[128,128]{1,0:T(8,128)(2,1)S(1)}, bf16[128,128]{1,0:T(8,128)(2,1)S(1)}, u32[]{:S(2)}, u32[]{:S(2)}) collective-permute-start(bf16[128,128]{1,0:T(8,128)(2,1)S(1)} %convert_element_type.219), channel_id=1, source_target_pairs={{0,1},{1,0},{2,3},{3,2},{4,5},{5,4},{6,7},{7,6},{8,9},{9,8},{10,11... | collective-permute-start | bytes 98312 | tf_op jit(solution)/shard_map/while/body/ppermute | solution.py:229
  132.0 4.2 %body.30 = (bf16[64,2048]{1,0:T(8,128)(2,1)S(1)}, bf16[64,2048]{1,0:T(8,128)(2,1)S(1)}, bf16[64,2048]{1,0:T(8,128)(2,1)S(1)}, bf16[64,2048]{1,0:T(8,128)(2,1)S(1)}) custom-call(s32[8]{0:T(128)S(1)} %constant_dynamic-update-slice_fusion.2.pos, f32[128,128]{1,0:T(8,128)S(1)} %convert_add_fusion.6.total, s8[256,1024]{1,0:T(32,128)(4,1)S(1)} %body.28.table, ...), custom_call_target="tpu_custom_call" | custom-call | flops 1100000000 | bytes 8000000 | tf_op jit(solution)/shard_map/while/body/pallas_call | solution.py:323
  136.3 3.1 %collective-permute-start.6 = (bf16[64,2048]{1,0:T(8,128)(2,1)S(1)}, bf16[64,2048]{1,0:T(8,128)(2,1)S(1)}, u32[]{:S(2)}, u32[]{:S(2)}) collective-permute-start(bf16[64,2048]{1,0:T(8,128)(2,1)S(1)} %get-tuple-element.403), channel_id=1, source_target_pairs={{0,128},{64,192},{128,0},{192,64},{1,129},{65,193},{129,1},{193,65... | collective-permute-start | bytes 786440 | tf_op jit(solution)/shard_map/while/body/ppermute | solution.py:233
  139.3 4.4 %collective-permute-done.5.p1 = bf16[64,2048]{1,0:T(8,128)(2,1)S(1)} collective-permute-done((bf16[64,2048]{1,0:T(8,128)(2,1)S(1)}, bf16[64,2048]{1,0:T(8,128)(2,1)S(1)}, u32[]{:S(2)}, u32[]{:S(2)}) %collective-permute-start.5) | collective-permute-done | bytes 262176 | tf_op jit(solution)/shard_map/while/body/ppermute | solution.py:233
  143.8 6.0 %collective-permute-done.6.p2 = bf16[64,2048]{1,0:T(8,128)(2,1)S(1)} collective-permute-done((bf16[64,2048]{1,0:T(8,128)(2,1)S(1)}, bf16[64,2048]{1,0:T(8,128)(2,1)S(1)}, u32[]{:S(2)}, u32[]{:S(2)}) %collective-permute-start.6) | collective-permute-done | bytes 262176 | tf_op jit(solution)/shard_map/while/body/ppermute | solution.py:233
  153.5 6.7 %all-to-all-start.2 = ((bf16[16,8,2048]{2,1,0:T(8,128)(2,1)}), bf16[16,8,2048]{2,1,0:T(8,128)(2,1)S(1)}, u32[]{:S(2)}, u32[]{:S(2)}) async-start(bf16[16,8,2048]{2,1,0:T(8,128)(2,1)} %convert_bitcast_fusion), calls=%async_computation.2 | async-start | bytes 1048576 | tf_op jit(solution)/shard_map/all_to_all | solution.py:336
  161.0 3.4 %collective-permute-start.30 = (bf16[8,512]{1,0:T(8,128)(2,1)S(1)}, bf16[8,512]{1,0:T(8,128)(2,1)S(1)}, u32[]{:S(2)}, u32[]{:S(2)}) collective-permute-start(bf16[8,512]{1,0:T(8,128)(2,1)S(1)} %get-tuple-element.293), channel_id=1, source_target_pairs={{0,192},{64,0},{128,64},{192,128},{1,193},{65,1},{129,65},{193,129... | collective-permute-start | bytes 24584 | tf_op jit(solution)/shard_map/ppermute | solution.py:233
  165.2 3.2 %collective-permute-done.29 = bf16[8,512]{1,0:T(8,128)(2,1)S(1)} collective-permute-done((bf16[8,512]{1,0:T(8,128)(2,1)S(1)}, bf16[8,512]{1,0:T(8,128)(2,1)S(1)}, u32[]{:S(2)}, u32[]{:S(2)}) %collective-permute-start.29) | collective-permute-done | bytes 8224 | tf_op jit(solution)/shard_map/ppermute | solution.py:233
  168.5 6.2 %all-to-all-done.2 = bf16[16,8,2048]{2,1,0:T(8,128)(2,1)S(1)} async-done(((bf16[16,8,2048]{2,1,0:T(8,128)(2,1)}), bf16[16,8,2048]{2,1,0:T(8,128)(2,1)S(1)}, u32[]{:S(2)}, u32[]{:S(2)}) %all-to-all-start.2) | async-done | bytes 524320 | tf_op jit(solution)/shard_map/all_to_all | solution.py:336
  175.5 3.2 %collective-permute-start.31 = (f32[2,8]{1,0:T(2,128)S(1)}, f32[2,8]{1,0:T(2,128)S(1)}, u32[]{:S(2)}, u32[]{:S(2)}) collective-permute-start(f32[2,8]{1,0:T(2,128)S(1)} %pad_maximum_fusion.2), channel_id=1, source_target_pairs={{0,1},{1,0},{2,3},{3,2},{4,5},{5,4},{6,7},{7,6},{8,9},{9,8},{10,11... | collective-permute-start | bytes 200 | tf_op jit(solution)/shard_map/ppermute | solution.py:229
  (128 shorter events, 64.0 us)
Async XLA Ops:
  0.6 17.7 %collective-permute-start.13 = (bf16[512,896]{1,0:T(8,128)(2,1)}, bf16[512,896]{1,0:T(8,128)(2,1)S(1)}, u32[]{:S(2)}, u32[]{:S(2)}) collective-permute-start(bf16[512,896]{1,0:T(8,128)(2,1)} %bitcast.47), channel_id=1, source_target_pairs={{0,1},{1,0},{2,3},{3,2},{4,5},{5,4},{6,7},{7,6},{8,9},{9,8},{10,11... | collective-permute-start | bytes 2752520 | tf_op jit(solution)/shard_map/ppermute | solution.py:229
  4.0 21.9 %collective-permute-start.18 = (bf16[512,896]{1,0:T(8,128)(2,1)}, bf16[512,896]{1,0:T(8,128)(2,1)S(1)}, u32[]{:S(2)}, u32[]{:S(2)}) collective-permute-start(bf16[512,896]{1,0:T(8,128)(2,1)} %bitcast.45), channel_id=1, source_target_pairs={{0,1},{1,0},{2,3},{3,2},{4,5},{5,4},{6,7},{7,6},{8,9},{9,8},{10,11... | collective-permute-start | bytes 2752520 | tf_op jit(solution)/shard_map/ppermute | solution.py:229
  9.1 6.6 %collective-permute-start.10 = (bf16[64,1024]{1,0:T(8,128)(2,1)S(1)}, bf16[64,1024]{1,0:T(8,128)(2,1)S(1)}, u32[]{:S(2)}, u32[]{:S(2)}) collective-permute-start(bf16[64,1024]{1,0:T(8,128)(2,1)S(1)} %get-tuple-element.229), channel_id=1, source_target_pairs={{0,64},{64,128},{128,192},{192,0},{1,65},{65,129},{129,193},{193,1... | collective-permute-start | bytes 393224 | tf_op jit(solution)/shard_map/ppermute | solution.py:233
  9.2 8.4 %collective-permute-start.11 = (bf16[64,1024]{1,0:T(8,128)(2,1)S(1)}, bf16[64,1024]{1,0:T(8,128)(2,1)S(1)}, u32[]{:S(2)}, u32[]{:S(2)}) collective-permute-start(bf16[64,1024]{1,0:T(8,128)(2,1)S(1)} %get-tuple-element.230), channel_id=1, source_target_pairs={{0,128},{64,192},{128,0},{192,64},{1,129},{65,193},{129,1},{193,65... | collective-permute-start | bytes 393224 | tf_op jit(solution)/shard_map/ppermute | solution.py:233
  11.4 6.9 %collective-permute-start.12 = (bf16[64,1024]{1,0:T(8,128)(2,1)S(1)}, bf16[64,1024]{1,0:T(8,128)(2,1)S(1)}, u32[]{:S(2)}, u32[]{:S(2)}) collective-permute-start(bf16[64,1024]{1,0:T(8,128)(2,1)S(1)} %get-tuple-element.231), channel_id=1, source_target_pairs={{0,192},{64,0},{128,64},{192,128},{1,193},{65,1},{129,65},{193,129... | collective-permute-start | bytes 393224 | tf_op jit(solution)/shard_map/ppermute | solution.py:233
  20.8 9.9 %collective-permute-start.16 = (bf16[64,1024]{1,0:T(8,128)(2,1)S(1)}, bf16[64,1024]{1,0:T(8,128)(2,1)S(1)}, u32[]{:S(2)}, u32[]{:S(2)}) collective-permute-start(bf16[64,1024]{1,0:T(8,128)(2,1)S(1)} %get-tuple-element.237), channel_id=1, source_target_pairs={{0,192},{64,0},{128,64},{192,128},{1,193},{65,1},{129,65},{193,129... | collective-permute-start | bytes 393224 | tf_op jit(solution)/shard_map/ppermute | solution.py:233
  24.2 8.3 %collective-permute-start.15 = (bf16[64,1024]{1,0:T(8,128)(2,1)S(1)}, bf16[64,1024]{1,0:T(8,128)(2,1)S(1)}, u32[]{:S(2)}, u32[]{:S(2)}) collective-permute-start(bf16[64,1024]{1,0:T(8,128)(2,1)S(1)} %get-tuple-element.236), channel_id=1, source_target_pairs={{0,128},{64,192},{128,0},{192,64},{1,129},{65,193},{129,1},{193,65... | collective-permute-start | bytes 393224 | tf_op jit(solution)/shard_map/ppermute | solution.py:233
  24.2 9.5 %collective-permute-start.14 = (bf16[64,1024]{1,0:T(8,128)(2,1)S(1)}, bf16[64,1024]{1,0:T(8,128)(2,1)S(1)}, u32[]{:S(2)}, u32[]{:S(2)}) collective-permute-start(bf16[64,1024]{1,0:T(8,128)(2,1)S(1)} %get-tuple-element.235), channel_id=1, source_target_pairs={{0,64},{64,128},{128,192},{192,0},{1,65},{65,129},{129,193},{193,1... | collective-permute-start | bytes 393224 | tf_op jit(solution)/shard_map/ppermute | solution.py:233
  24.8 23.5 %collective-permute-start.26 = (bf16[896,512]{1,0:T(8,128)(2,1)}, bf16[896,512]{1,0:T(8,128)(2,1)S(1)}, u32[]{:S(2)}, u32[]{:S(2)}) collective-permute-start(bf16[896,512]{1,0:T(8,128)(2,1)} %bitcast.49), channel_id=1, source_target_pairs={{0,1},{1,0},{2,3},{3,2},{4,5},{5,4},{6,7},{7,6},{8,9},{9,8},{10,11... | collective-permute-start | bytes 2752520 | tf_op jit(solution)/shard_map/ppermute | solution.py:229
  28.4 5.9 %collective-permute-start.21 = (bf16[64,896]{1,0:T(8,128)(2,1)S(1)}, bf16[64,896]{1,0:T(8,128)(2,1)S(1)}, u32[]{:S(2)}, u32[]{:S(2)}) collective-permute-start(bf16[64,896]{1,0:T(8,128)(2,1)S(1)} %get-tuple-element.242), channel_id=1, source_target_pairs={{0,192},{64,0},{128,64},{192,128},{1,193},{65,1},{129,65},{193,129... | collective-permute-start | bytes 344072 | tf_op jit(solution)/shard_map/ppermute | solution.py:233
  30.7 6.0 %collective-permute-start.20 = (bf16[64,896]{1,0:T(8,128)(2,1)S(1)}, bf16[64,896]{1,0:T(8,128)(2,1)S(1)}, u32[]{:S(2)}, u32[]{:S(2)}) collective-permute-start(bf16[64,896]{1,0:T(8,128)(2,1)S(1)} %get-tuple-element.241), channel_id=1, source_target_pairs={{0,128},{64,192},{128,0},{192,64},{1,129},{65,193},{129,1},{193,65... | collective-permute-start | bytes 344072 | tf_op jit(solution)/shard_map/ppermute | solution.py:233
  32.5 6.9 %collective-permute-start.19 = (bf16[64,896]{1,0:T(8,128)(2,1)S(1)}, bf16[64,896]{1,0:T(8,128)(2,1)S(1)}, u32[]{:S(2)}, u32[]{:S(2)}) collective-permute-start(bf16[64,896]{1,0:T(8,128)(2,1)S(1)} %get-tuple-element.240), channel_id=1, source_target_pairs={{0,64},{64,128},{128,192},{192,0},{1,65},{65,129},{129,193},{193,1... | collective-permute-start | bytes 344072 | tf_op jit(solution)/shard_map/ppermute | solution.py:233
  33.7 6.7 %collective-permute-start.17 = (bf16[64,1024]{1,0:T(8,128)(2,1)S(1)}, bf16[64,1024]{1,0:T(8,128)(2,1)S(1)}, u32[]{:S(2)}, u32[]{:S(2)}) collective-permute-start(bf16[64,1024]{1,0:T(8,128)(2,1)S(1)} %fusion.3), channel_id=1, source_target_pairs={{0,2},{2,0},{1,3},{3,1},{4,6},{6,4},{5,7},{7,5},{8,10},{10,8},{9,1... | collective-permute-start | bytes 393224 | tf_op jit(solution)/shard_map/ppermute | solution.py:229
  43.4 5.1 %collective-permute-start.23 = (bf16[64,896]{1,0:T(8,128)(2,1)S(1)}, bf16[64,896]{1,0:T(8,128)(2,1)S(1)}, u32[]{:S(2)}, u32[]{:S(2)}) collective-permute-start(bf16[64,896]{1,0:T(8,128)(2,1)S(1)} %multiply_convert_fusion.refs_0_), channel_id=1, source_target_pairs={{0,64},{64,128},{128,192},{192,0},{1,65},{65,129},{129,193},{193,1... | collective-permute-start | bytes 344072 | tf_op jit(solution)/shard_map/ppermute | solution.py:233
  43.7 6.8 %collective-permute-start.24 = (bf16[64,896]{1,0:T(8,128)(2,1)S(1)}, bf16[64,896]{1,0:T(8,128)(2,1)S(1)}, u32[]{:S(2)}, u32[]{:S(2)}) collective-permute-start(bf16[64,896]{1,0:T(8,128)(2,1)S(1)} %multiply_convert_fusion.refs_0_), channel_id=1, source_target_pairs={{0,128},{64,192},{128,0},{192,64},{1,129},{65,193},{129,1},{193,65... | collective-permute-start | bytes 344072 | tf_op jit(solution)/shard_map/ppermute | solution.py:233
  52.7 25.4 %all-to-all-start = ((bf16[16,16,1024]{2,1,0:T(8,128)(2,1)}), bf16[16,16,1024]{2,1,0:T(8,128)(2,1)S(1)}, u32[]{:S(2)}, u32[]{:S(2)}) async-start(bf16[16,16,1024]{2,1,0:T(8,128)(2,1)} %bitcast.10), calls=%async_computation | async-start | bytes 1048576 | tf_op jit(solution)/shard_map/all_to_all | solution.py:286
  83.6 20.1 %all-to-all-start.1 = ((bf16[16,32,512]{2,1,0:T(8,128)(2,1)}), bf16[16,32,512]{2,1,0:T(8,128)(2,1)}, u32[]{:S(2)}, u32[]{:S(2)}) async-start(bf16[16,32,512]{2,1,0:T(8,128)(2,1)} %broadcast_in_dim.18), calls=%async_computation.1 | async-start | bytes 1048576 | tf_op jit(solution)/shard_map/all_to_all | solution.py:294
  105.6 10.0 %collective-permute-start = (bf16[256,512]{1,0:T(8,128)(2,1)S(1)}, bf16[256,512]{1,0:T(8,128)(2,1)S(1)}, u32[]{:S(2)}, u32[]{:S(2)}) collective-permute-start(bf16[256,512]{1,0:T(8,128)(2,1)S(1)} %get-tuple-element.393), channel_id=1, source_target_pairs={{0,64},{64,128},{128,192},{192,0},{1,65},{65,129},{129,193},{193,1... | collective-permute-start | bytes 786440 | tf_op jit(solution)/shard_map/while/body/ppermute | solution.py:233
  105.9 13.2 %collective-permute-start.1 = (bf16[256,512]{1,0:T(8,128)(2,1)S(1)}, bf16[256,512]{1,0:T(8,128)(2,1)S(1)}, u32[]{:S(2)}, u32[]{:S(2)}) collective-permute-start(bf16[256,512]{1,0:T(8,128)(2,1)S(1)} %get-tuple-element.394), channel_id=1, source_target_pairs={{0,128},{64,192},{128,0},{192,64},{1,129},{65,193},{129,1},{193,65... | collective-permute-start | bytes 786440 | tf_op jit(solution)/shard_map/while/body/ppermute | solution.py:233
  110.2 9.9 %collective-permute-start.2 = (bf16[256,512]{1,0:T(8,128)(2,1)S(1)}, bf16[256,512]{1,0:T(8,128)(2,1)S(1)}, u32[]{:S(2)}, u32[]{:S(2)}) collective-permute-start(bf16[256,512]{1,0:T(8,128)(2,1)S(1)} %get-tuple-element.395), channel_id=1, source_target_pairs={{0,192},{64,0},{128,64},{192,128},{1,193},{65,1},{129,65},{193,129... | collective-permute-start | bytes 786440 | tf_op jit(solution)/shard_map/while/body/ppermute | solution.py:233
  136.2 7.6 %collective-permute-start.5 = (bf16[64,2048]{1,0:T(8,128)(2,1)S(1)}, bf16[64,2048]{1,0:T(8,128)(2,1)S(1)}, u32[]{:S(2)}, u32[]{:S(2)}) collective-permute-start(bf16[64,2048]{1,0:T(8,128)(2,1)S(1)} %get-tuple-element.402), channel_id=1, source_target_pairs={{0,64},{64,128},{128,192},{192,0},{1,65},{65,129},{129,193},{193,1... | collective-permute-start | bytes 786440 | tf_op jit(solution)/shard_map/while/body/ppermute | solution.py:233
  136.3 13.5 %collective-permute-start.6 = (bf16[64,2048]{1,0:T(8,128)(2,1)S(1)}, bf16[64,2048]{1,0:T(8,128)(2,1)S(1)}, u32[]{:S(2)}, u32[]{:S(2)}) collective-permute-start(bf16[64,2048]{1,0:T(8,128)(2,1)S(1)} %get-tuple-element.403), channel_id=1, source_target_pairs={{0,128},{64,192},{128,0},{192,64},{1,129},{65,193},{129,1},{193,65... | collective-permute-start | bytes 786440 | tf_op jit(solution)/shard_map/while/body/ppermute | solution.py:233
  139.3 11.5 %collective-permute-start.7 = (bf16[64,2048]{1,0:T(8,128)(2,1)S(1)}, bf16[64,2048]{1,0:T(8,128)(2,1)S(1)}, u32[]{:S(2)}, u32[]{:S(2)}) collective-permute-start(bf16[64,2048]{1,0:T(8,128)(2,1)S(1)} %get-tuple-element.404), channel_id=1, source_target_pairs={{0,192},{64,0},{128,64},{192,128},{1,193},{65,1},{129,65},{193,129... | collective-permute-start | bytes 786440 | tf_op jit(solution)/shard_map/while/body/ppermute | solution.py:233
  153.5 21.2 %all-to-all-start.2 = ((bf16[16,8,2048]{2,1,0:T(8,128)(2,1)}), bf16[16,8,2048]{2,1,0:T(8,128)(2,1)S(1)}, u32[]{:S(2)}, u32[]{:S(2)}) async-start(bf16[16,8,2048]{2,1,0:T(8,128)(2,1)} %convert_bitcast_fusion), calls=%async_computation.2 | async-start | bytes 1048576 | tf_op jit(solution)/shard_map/all_to_all | solution.py:336
  (21 other events, 247.8 us)
